TPU v7x, 32 devices: a whole 2x2x4 slice. The times are simulated.
32 devices in a mesh: ctx: 16 (over z, y, x), tp: 2 (over core).
Axes of the slice: x: 2, y: 2, z: 4, core: 2. Of those that a mesh axis runs over, the one named last changes fastest.
Arguments:
- tokens: bfloat16 [8192, 5120], P('ctx', 'tp'), may hold values from -6 to 6
- norm_gain: float32 [5120], replicated, may hold values from 0.1 to 1.9
- w_query: bfloat16 [5120, 5120], P('ctx', 'tp'), may hold values from -0.078125 to 0.078125
- cache_keys: bfloat16 [8192, 1024], P('ctx', 'tp'), may hold values from -100 to 100
- cache_values: bfloat16 [8192, 1024], P('ctx', 'tp'), may hold values from -6 to 6
- doc_start: int32 [8192], P('ctx'), may hold values from 0 to 8191, as said below
- tile_mask: int32 [64, 64], P('ctx'), may hold values from 0 to 1, as said below
Outputs:
- attended: bfloat16 [8192, 5120], P('ctx', 'tp')
Inputs may be any that keep to these rules, and one draw needn't show every extreme that they name: Documents are contiguous: doc_start is the same within a document and i - 2048 < doc_start[i] <= i; some document has exactly 2048 tokens. `tile_mask`: every diagonal tile is 1.
All inputs are finite; a program needn't handle non-finite values.
Results may differ from a plain program's by a relative error of at most 0.012.
The roundings to bfloat16 on the way count: a program that leaves them out, or rounds other values in their place, can miss the bound.
Values may be sent and summed in bfloat16 or wider, within the bound.
No kernel may reach another device: no remote copies, remote signals or barrier semaphores. Data moves between devices by JAX's collectives and lax.ppermute only.
A program may use at most 256 MiB of HBM per device.

v0:
```python
import jax
import jax.numpy as jnp
from jax import lax
from jax.sharding import PartitionSpec as P

HD = 128
TILE = 128
MAXDOC = 2048


epsilon = 1e-05


def shifted(block, axis, distance):
    devices = range(lax.axis_size(axis))
    route = [(i - distance, i) for i in devices if i - distance in devices]
    return lax.ppermute(block, axis, route)


def on_device(tokens, norm_gain, w_query, cache_keys, cache_values, doc_start, tile_mask):
    gathered = lax.all_gather(tokens, "tp", axis=1, tiled=True)
    float_tokens = gathered.astype(jnp.float32)
    inverse = lax.rsqrt(jnp.mean(float_tokens * float_tokens, axis=-1, keepdims=True) + epsilon)
    normed = (float_tokens * inverse * norm_gain).astype(jnp.bfloat16)
    tok_rows = tokens.shape[0]
    columns = w_query.shape[1]
    queries = jnp.dot(
        normed,
        lax.all_gather(w_query, "ctx", axis=0, tiled=True),
        preferred_element_type=jnp.float32,
    ).astype(jnp.bfloat16)
    kv_heads = cache_keys.shape[1] // HD
    q_heads = columns // HD
    group_size = q_heads // kv_heads
    query_four = queries.reshape(tok_rows, kv_heads, group_size, HD)
    shard_index = lax.axis_index("ctx")
    query_pos = shard_index * tok_rows + jnp.arange(tok_rows, dtype=jnp.int32)
    tiles_dev = tok_rows // TILE
    score_scale = 1.0 / HD**0.5

    def attend(running, kv_block, distance):
        key_pos = (shard_index - distance) * tok_rows + jnp.arange(tok_rows, dtype=jnp.int32)
        tile_block = lax.dynamic_slice_in_dim(
            tile_mask, jnp.maximum(shard_index - distance, 0) * tiles_dev, tiles_dev, 1
        )
        expanded = jnp.repeat(jnp.repeat(tile_block, TILE, axis=0), TILE, axis=1)
        visible = (
            (key_pos[None, :] <= query_pos[:, None])
            & (key_pos[None, :] >= doc_start[:, None])
            & (expanded == 1)
        )
        row_max, weight_sum, summed = running
        key_three = kv_block[0].reshape(tok_rows, kv_heads, HD)
        value_three = kv_block[1].reshape(tok_rows, kv_heads, HD)
        scores = (
            jnp.einsum("qkgd,pkd->kgqp", query_four, key_three, preferred_element_type=jnp.float32)
            * score_scale
        )
        masked = jnp.where(visible, scores, -1e30)
        new_max = jnp.maximum(row_max, jnp.max(masked, axis=-1))
        rescale = jnp.exp(row_max - new_max)
        weights = jnp.where(visible, jnp.exp(masked - new_max[..., None]), 0.0)
        weight_sum = weight_sum * rescale + jnp.sum(weights, axis=-1)
        product = jnp.einsum(
            "kgqp,pkd->kgqd",
            weights.astype(jnp.bfloat16),
            value_three,
            preferred_element_type=jnp.float32,
        )
        summed = summed * rescale[..., None] + product
        return (new_max, weight_sum, summed)

    running = (
        jnp.full((kv_heads, group_size, tok_rows), -1e30, jnp.float32),
        jnp.zeros((kv_heads, group_size, tok_rows), jnp.float32),
        jnp.zeros((kv_heads, group_size, tok_rows, HD), jnp.float32),
    )
    stacked = jnp.stack((cache_keys, cache_values))
    running = attend(running, stacked, 0)
    reach = (MAXDOC + tok_rows - 2) // tok_rows
    moving = stacked
    for distance in range(1, reach + 1):
        moving = shifted(moving, "ctx", 1)
        running = attend(running, moving, distance)
    row_max, weight_sum, summed = running
    result = summed / weight_sum[..., None]
    return jnp.transpose(result, (2, 0, 1, 3)).reshape(tok_rows, columns).astype(jnp.bfloat16)


def solution(mesh):
    return jax.shard_map(
        on_device,
        mesh=mesh,
        in_specs=(
            P("ctx", "tp"),
            P(),
            P("ctx", "tp"),
            P("ctx", "tp"),
            P("ctx", "tp"),
            P("ctx"),
            P("ctx", None),
        ),
        out_specs=P("ctx", "tp"),
        check_vma=False,
    )
```

profile of v0, /device:TPU:0, one launch (start us, length us, event | category | flops | bytes accessed | tf_op | source)
XLA Modules:
  0.0 551.6 jit_solution(6505299703410204181)
XLA Ops:
  8.0 1.3 copy.77
  9.3 1.4 copy.37
  10.8 4.9 collective-permute-start
  15.7 22.3 %collective-permute-done = bf16[2,512,512]{1,2,0:T(8,128)(2,1)S(1)} collective-permute-done((bf16[2,512,512]{1,2,0:T(8,128)(2,1)S(1)}, bf16[2,512,512]{1,2,0:T(8,128)(2,1)S(1)}, u32[]{:S(2)}, u32[]{:S(2)}) %collective-permute-start) | collective-permute-done | bytes 1048608 | tf_op jit(solution)/shard_map/ppermute | solution.py:17
  38.1 4.4 collective-permute-start.1
  43.7 31.4 %collective-permute-done.1 = bf16[2,512,512]{1,2,0:T(8,128)(2,1)S(1)} collective-permute-done((bf16[2,512,512]{1,2,0:T(8,128)(2,1)S(1)}, bf16[2,512,512]{1,2,0:T(8,128)(2,1)S(1)}, u32[]{:S(2)}, u32[]{:S(2)}) %collective-permute-start.1) | collective-permute-done | bytes 1048608 | tf_op jit(solution)/shard_map/ppermute | solution.py:17
  75.1 5.4 collective-permute-start.2
  81.3 20.2 %collective-permute-done.2 = bf16[2,512,512]{1,2,0:T(8,128)(2,1)} collective-permute-done((bf16[2,512,512]{1,2,0:T(8,128)(2,1)S(1)}, bf16[2,512,512]{1,2,0:T(8,128)(2,1)}, u32[]{:S(2)}, u32[]{:S(2)}) %collective-permute-start.2) | collective-permute-done | bytes 1048608 | tf_op jit(solution)/shard_map/ppermute | solution.py:17
  101.5 5.5 %collective-permute-start.3 = (bf16[2,512,512]{1,2,0:T(8,128)(2,1)}, bf16[2,512,512]{1,2,0:T(8,128)(2,1)}, u32[]{:S(2)}, u32[]{:S(2)}) collective-permute-start(bf16[2,512,512]{1,2,0:T(8,128)(2,1)} %collective-permute-done.2), channel_id=1, source_target_pairs={{0,2},{2,4},{4,6},{6,8},{8,10},{10,12},{12,14},{14,16},{16,18},{18... | collective-permute-start | bytes 3145736 | tf_op jit(solution)/shard_map/ppermute | solution.py:17
  107.1 2.0 reshape_squeeze_stack.6
  109.1 2.7 bitcast_and_fusion.4
  113.9 2.3 fusion.82
  116.2 31.2 %collective-permute-done.3 = bf16[2,512,512]{1,2,0:T(8,128)(2,1)} collective-permute-done((bf16[2,512,512]{1,2,0:T(8,128)(2,1)}, bf16[2,512,512]{1,2,0:T(8,128)(2,1)}, u32[]{:S(2)}, u32[]{:S(2)}) %collective-permute-start.3) | collective-permute-done | bytes 1048608 | tf_op jit(solution)/shard_map/ppermute | solution.py:17
  147.3 2.3 fusion.79
  149.6 3.6 fusion.16
  153.2 220.1 %all-gather.5.cloned.1.call-done = bf16[5120,2560]{1,0:T(8,128)(2,1)} async-done(((bf16[320,2560]{1,0:T(8,128)(2,1)}), bf16[5120,2560]{1,0:T(8,128)(2,1)}) %all-gather.5.cloned.1.call-update) | async-done | bytes 26214416 | tf_op jit(solution)/shard_map/all_gather | solution.py:29
  373.4 21.2 %fusion.45 = bf16[512,2560]{1,0:T(8,128)(2,1)} fusion(bf16[5120,2560]{1,0:T(8,128)(2,1)} %all-gather.5.cloned.1.call-done, bf16[512,5120]{1,0:T(8,128)(2,1)} %all-gather.3.cloned.1.call-done, f32[5120]{0:T(1024)S(1)} %copy-done.24, f32[512]{0:T(512)S(1)} %add_rsqrt_fusion), kind=kOutput, calls=%fused_computation.57 | convolution fusion | flops 13433569280 | bytes 34101248 | tf_op jit(solution)/shard_map/dot_general | solution.py:27
  394.6 3.0 copy.31
  397.6 5.0 bitcast_reduce_fusion
  402.7 9.5 %fusion.2 = (f32[4,5,512]{2,1,0:T(8,128)S(1)}, f32[4,512,512,5]{2,1,3,0:T(8,128)}) fusion(pred[512,512]{0,1:T(8,128)(4,1)S(1)} %copy-done.1, bf16[512,4,128,1]{0,2,3,1:T(8,128)(2,1)S(1)} %bitcast.305, bf16[512,4,5,128]{0,3,2,1:T(8,128)(2,1)S(1)} %bitcast.295), kind=kOutput, calls=%fused_computation.13 | convolution fusion | flops 1357895680 | bytes 24420352 | tf_op jit(solution)/shard_map/qkgd,pkd->kgqp/dot_general | solution.py:56
  412.2 10.3 %fusion.3 = (f32[4,5,512]{2,1,0:T(8,128)S(1)}, f32[4,512,512,5]{2,1,3,0:T(8,128)}) fusion(pred[512,512]{0,1:T(8,128)(4,1)S(1)} %copy-done.3, bf16[512,4,128,1]{0,2,3,1:T(8,128)(2,1)S(1)} %bitcast.306, bf16[512,4,5,128]{0,3,2,1:T(8,128)(2,1)S(1)} %bitcast.296), kind=kOutput, calls=%fused_computation.14 | convolution fusion | flops 1357895680 | bytes 24420352 | tf_op jit(solution)/shard_map/qkgd,pkd->kgqp/dot_general | solution.py:56
  422.5 8.9 %fusion.4 = (f32[4,5,512]{2,1,0:T(8,128)S(1)}, f32[4,512,512,5]{2,1,3,0:T(8,128)}) fusion(pred[512,512]{0,1:T(8,128)(4,1)S(1)} %get-tuple-element.27, bf16[512,4,128,1]{0,2,3,1:T(8,128)(2,1)S(1)} %bitcast.307, bf16[512,4,5,128]{0,3,2,1:T(8,128)(2,1)S(1)} %bitcast.297), kind=kOutput, calls=%fused_computation.15 | convolution fusion | flops 1357895680 | bytes 24420352 | tf_op jit(solution)/shard_map/qkgd,pkd->kgqp/dot_general | solution.py:56
  431.4 9.0 %fusion.5 = (f32[4,5,512]{2,1,0:T(8,128)S(1)}, f32[4,512,512,5]{2,1,3,0:T(8,128)}) fusion(pred[512,512]{0,1:T(8,128)(4,1)S(1)} %get-tuple-element.28, bf16[512,4,128,1]{0,2,3,1:T(8,128)(2,1)S(1)} %bitcast.308, bf16[512,4,5,128]{0,3,2,1:T(8,128)(2,1)S(1)} %bitcast.298), kind=kOutput, calls=%fused_computation.16 | convolution fusion | flops 1357895680 | bytes 24420352 | tf_op jit(solution)/shard_map/qkgd,pkd->kgqp/dot_general | solution.py:56
  441.1 5.8 %fusion.14 = f32[4,5,512]{2,1,0:T(8,128)} fusion(f32[4,512,5,512]{1,3,2,0:T(8,128)S(1)} %get-tuple-element.43, f32[4,5,512]{2,1,0:T(8,128)S(1)} %get-tuple-element.23, pred[512,512]{0,1:T(8,128)(4,1)S(1)} %get-tuple-element.24), kind=kLoop, calls=%fused_computation.25 | loop fusion | flops 26204160 | bytes 21315584 | tf_op jit(solution)/shard_map/reduce_sum | solution.py:63
  447.0 11.4 %fusion.19 = f32[4,5,512,128]{2,3,1,0:T(8,128)} fusion(bf16[512,4,128,1]{0,2,3,1:T(8,128)(2,1)S(1)} %bitcast.310, f32[4,512,5,512]{1,3,2,0:T(8,128)} %copy-done, f32[4,5,512]{2,1,0:T(8,128)S(1)} %get-tuple-element.23, pred[512,512]{0,1:T(8,128)(4,1)S(1)} %get-tuple-element.24), kind=kOutput, calls=%fused_computation.32 | convolution fusion | flops 1368391680 | bytes 27041792 | tf_op jit(solution)/shard_map/kgqp,pkd->kgqd/dot_general | solution.py:64
  458.5 11.6 %fusion.25 = f32[4,5,512,128]{2,3,1,0:T(8,128)} fusion(bf16[512,4,128,1]{0,2,3,1:T(8,128)(2,1)} %bitcast.315, f32[4,512,512,5]{2,1,3,0:T(8,128)} %get-tuple-element.39, f32[4,5,512]{2,1,0:T(8,128)S(1)} %get-tuple-element.11, pred[512,512]{0,1:T(8,128)(4,1)S(1)} %copy-done.4), kind=kOutput, calls=%fused_computation.35 | convolution fusion | flops 1368391680 | bytes 27041792 | tf_op jit(solution)/shard_map/kgqp,pkd->kgqd/dot_general | solution.py:64
  473.6 13.6 %fusion.6 = (f32[4,5,512]{2,1,0:T(8,128)}, f32[4,5,512]{2,1,0:T(8,128)}) fusion(f32[4,512,512,5]{2,1,3,0:T(8,128)S(1)} %bitcast.302, f32[4,5,512]{2,1,0:T(8,128)S(1)} %get-tuple-element.12, pred[512,512]{0,1:T(8,128)(4,1)S(1)} %copy-done.2, f32[4,5,512]{2,1,0:T(8,128)S(1)} %get-tuple-element.11, f32[4,512,512,5]{2,1,3,0:T(8,128)} %get-tuple-element.39, ...), kind=kLoop, calls=%fused_computation.17 | loop fusion | flops 52408320 | bytes 42631168 | tf_op jit(solution)/shard_map/reduce_sum | solution.py:63
  487.2 8.7 %fusion.27 = f32[4,5,512,128]{2,3,1,0:T(8,128)} fusion(bf16[512,4,128,1]{0,2,3,1:T(8,128)(2,1)} %bitcast.313, f32[4,512,512,5]{2,1,3,0:T(8,128)S(1)} %bitcast.302, f32[4,5,512]{2,1,0:T(8,128)} %copy-done.23, pred[512,512]{0,1:T(8,128)(4,1)S(1)} %copy-done.2), kind=kOutput, calls=%fused_computation.36 | convolution fusion | flops 1368391680 | bytes 27041792 | tf_op jit(solution)/shard_map/kgqp,pkd->kgqd/dot_general | solution.py:64
  495.9 11.5 %fusion.23 = f32[4,5,512,128]{2,3,1,0:T(8,128)} fusion(bf16[512,4,128,1]{0,2,3,1:T(8,128)(2,1)S(1)} %bitcast.314, f32[4,512,512,5]{2,1,3,0:T(8,128)} %get-tuple-element.37, f32[4,5,512]{2,1,0:T(8,128)S(1)} %copy-done.22, pred[512,512]{0,1:T(8,128)(4,1)S(1)} %get-tuple-element.27), kind=kOutput, calls=%fused_computation.34 | convolution fusion | flops 1368391680 | bytes 27041792 | tf_op jit(solution)/shard_map/kgqp,pkd->kgqd/dot_general | solution.py:64
  510.8 12.9 %fusion.10 = (f32[4,5,512]{2,1,0:T(8,128)S(1)}, f32[4,5,512]{2,1,0:T(8,128)S(1)}) fusion(f32[4,512,512,5]{2,1,3,0:T(8,128)} %get-tuple-element.37, f32[4,5,512]{2,1,0:T(8,128)} %get-tuple-element.10, pred[512,512]{0,1:T(8,128)(4,1)S(1)} %get-tuple-element.27, f32[4,5,512]{2,1,0:T(8,128)S(1)} %copy-done.18, f32[4,512,512,5]{2,1,3,0:T(8,128)S(1)} %bitcast.300, ...), kind=kLoop, calls=%fused_computation.21 | loop fusion | flops 52408320 | bytes 42631168 | tf_op jit(solution)/shard_map/reduce_sum | solution.py:63
  524.5 17.0 %fusion.38 = bf16[512,4,5,128]{0,3,2,1:T(8,128)(2,1)S(1)} fusion(f32[4,5,512,128]{2,3,1,0:T(8,128)} %fusion.23, f32[4,5,512,128]{2,3,1,0:T(8,128)} %fusion.25, f32[4,5,512,128]{2,3,1,0:T(8,128)} %fusion.27, f32[4,5,512,128]{2,3,1,0:T(8,128)} %fusion.19, f32[512,4,5]{0,2,1:T(8,128)S(1)} %get-tuple-element.5, f32[512,4,5]{0,2,1:T(8,128)S(1)} %get-tuple-element.8, ...), kind=kOutput, calls=%fused_computation.46 | convolution fusion | flops 1382809600 | bytes 45637632 | tf_op jit(solution)/shard_map/kgqp,pkd->kgqd/dot_general | solution.py:64
  541.5 2.8 copy.54
  (104 shorter events, 13.9 us)
Async XLA Ops:
  6.5 366.8 %copy-start.24 = (f32[5120]{0:T(1024)S(1)}, f32[5120]{0:T(1024)}, u32[]{:S(2)}) copy-start(f32[5120]{0:T(1024)} %param.8) | copy-start | bytes 61444
  6.5 143.1 %all-gather.3.cloned.1.call-start = ((), (), s32[]{:S(2)}) async-start(), calls=%async_computation | async-start | bytes 7864320 | tf_op jit(solution)/shard_map/all_gather | solution.py:21
  7.3 366.1 %all-gather.5.cloned.1.call-start = ((), (), s32[]{:S(2)}) async-start(), calls=%async_computation.1 | async-start | bytes 27852800 | tf_op jit(solution)/shard_map/all_gather | solution.py:29
  9.3 364.1 %copy-start.9 = (bf16[512,512]{0,1:T(8,128)(2,1)}, bf16[512,512]{0,1:T(8,128)(2,1)S(1)}, u32[]{:S(2)}) copy-start(bf16[512,512]{0,1:T(8,128)(2,1)S(1)} %copy.77) | copy-start | bytes 1572868
  10.8 27.2 %collective-permute-start = (bf16[2,512,512]{1,2,0:T(8,128)(2,1)S(1)}, bf16[2,512,512]{1,2,0:T(8,128)(2,1)S(1)}, u32[]{:S(2)}, u32[]{:S(2)}) collective-permute-start(bf16[2,512,512]{1,2,0:T(8,128)(2,1)S(1)} %pad_maximum_fusion), channel_id=1, source_target_pairs={{0,2},{2,4},{4,6},{6,8},{8,10},{10,12},{12,14},{14,16},{16,18},{18... | collective-permute-start | bytes 3145736 | tf_op jit(solution)/shard_map/ppermute | solution.py:17
  38.1 37.1 %collective-permute-start.1 = (bf16[2,512,512]{1,2,0:T(8,128)(2,1)S(1)}, bf16[2,512,512]{1,2,0:T(8,128)(2,1)S(1)}, u32[]{:S(2)}, u32[]{:S(2)}) collective-permute-start(bf16[2,512,512]{1,2,0:T(8,128)(2,1)S(1)} %collective-permute-done), channel_id=1, source_target_pairs={{0,2},{2,4},{4,6},{6,8},{8,10},{10,12},{12,14},{14,16},{16,18},{18... | collective-permute-start | bytes 3145736 | tf_op jit(solution)/shard_map/ppermute | solution.py:17
  75.1 26.4 %collective-permute-start.2 = (bf16[2,512,512]{1,2,0:T(8,128)(2,1)S(1)}, bf16[2,512,512]{1,2,0:T(8,128)(2,1)}, u32[]{:S(2)}, u32[]{:S(2)}) collective-permute-start(bf16[2,512,512]{1,2,0:T(8,128)(2,1)S(1)} %collective-permute-done.1), channel_id=1, source_target_pairs={{0,2},{2,4},{4,6},{6,8},{8,10},{10,12},{12,14},{14,16},{16,18},{18... | collective-permute-start | bytes 3145736 | tf_op jit(solution)/shard_map/ppermute | solution.py:17
  101.5 45.8 %collective-permute-start.3 = (bf16[2,512,512]{1,2,0:T(8,128)(2,1)}, bf16[2,512,512]{1,2,0:T(8,128)(2,1)}, u32[]{:S(2)}, u32[]{:S(2)}) collective-permute-start(bf16[2,512,512]{1,2,0:T(8,128)(2,1)} %collective-permute-done.2), channel_id=1, source_target_pairs={{0,2},{2,4},{4,6},{6,8},{8,10},{10,12},{12,14},{14,16},{16,18},{18... | collective-permute-start | bytes 3145736 | tf_op jit(solution)/shard_map/ppermute | solution.py:17
  397.6 14.6 %copy-start.3 = (pred[512,512]{0,1:T(8,128)(4,1)S(1)}, pred[512,512]{0,1:T(8,128)(4,1)}, u32[]{:S(2)}) copy-start(pred[512,512]{0,1:T(8,128)(4,1)} %get-tuple-element.26) | copy-start | bytes 786436
  397.6 14.6 %copy-start.6 = (bf16[1,512,512]{1,2,0:T(8,128)(2,1)S(1)}, bf16[1,512,512]{1,2,0:T(8,128)(2,1)}, u32[]{:S(2)}) copy-start(bf16[1,512,512]{1,2,0:T(8,128)(2,1)} %get-tuple-element.18) | copy-start | bytes 1572868
  402.7 38.5 %copy-start = (f32[4,512,5,512]{1,3,2,0:T(8,128)}, f32[4,512,5,512]{1,3,2,0:T(8,128)S(1)}, u32[]{:S(2)}) copy-start(f32[4,512,5,512]{1,3,2,0:T(8,128)S(1)} %get-tuple-element.43) | copy-start | bytes 62914564
  402.7 19.8 %copy-start.7 = (bf16[1,512,512]{1,2,0:T(8,128)(2,1)S(1)}, bf16[1,512,512]{1,2,0:T(8,128)(2,1)}, u32[]{:S(2)}) copy-start(bf16[1,512,512]{1,2,0:T(8,128)(2,1)} %get-tuple-element.19) | copy-start | bytes 1572868
  412.2 19.3 %copy-start.8 = (bf16[1,512,512]{1,2,0:T(8,128)(2,1)S(1)}, bf16[1,512,512]{1,2,0:T(8,128)(2,1)}, u32[]{:S(2)}) copy-start(bf16[1,512,512]{1,2,0:T(8,128)(2,1)} %get-tuple-element.14) | copy-start | bytes 1572868
  422.5 17.9 %copy-start.11 = (f32[4,5,512]{2,1,0:T(8,128)}, f32[4,5,512]{2,1,0:T(8,128)S(1)}, u32[]{:S(2)}) copy-start(f32[4,5,512]{2,1,0:T(8,128)S(1)} %get-tuple-element.38) | copy-start | bytes 122884
  431.4 15.6 %copy-start.13 = (f32[4,5,512]{2,1,0:T(8,128)}, f32[4,5,512]{2,1,0:T(8,128)S(1)}, u32[]{:S(2)}) copy-start(f32[4,5,512]{2,1,0:T(8,128)S(1)} %get-tuple-element.36) | copy-start | bytes 122884
  431.4 15.6 %copy-start.10 = (bf16[512,512]{0,1:T(8,128)(2,1)S(1)}, bf16[512,512]{0,1:T(8,128)(2,1)}, u32[]{:S(2)}) copy-start(bf16[512,512]{0,1:T(8,128)(2,1)} %copy-done.9) | copy-start | bytes 1572868
  440.4 18.0 %copy-start.15 = (f32[4,5,512]{2,1,0:T(8,128)}, f32[4,5,512]{2,1,0:T(8,128)S(1)}, u32[]{:S(2)}) copy-start(f32[4,5,512]{2,1,0:T(8,128)S(1)} %get-tuple-element.34) | copy-start | bytes 122884
  441.1 28.9 %copy-start.23 = (f32[4,5,512]{2,1,0:T(8,128)}, f32[4,5,512]{2,1,0:T(8,128)S(1)}, u32[]{:S(2)}) copy-start(f32[4,5,512]{2,1,0:T(8,128)S(1)} %get-tuple-element.12) | copy-start | bytes 122884
  458.4 11.7 %slice-start.5 = ((s8[20971520]{0:T(1024)(128)(4,1)}), s8[4194304]{0:T(1024)(128)(4,1)S(1)}, s32[]{:S(2)}) async-start(s8[20971520]{0:T(1024)(128)(4,1)} %bitcast.301), calls=%async_computation.7 | async-start | bytes 8388608
  458.4 11.7 %copy-start.2 = (pred[512,512]{0,1:T(8,128)(4,1)S(1)}, pred[512,512]{0,1:T(8,128)(4,1)}, u32[]{:S(2)}) copy-start(pred[512,512]{0,1:T(8,128)(4,1)} %get-tuple-element.25) | copy-start | bytes 786436
  458.4 12.7 %slice-start.7 = ((s8[20971520]{0:T(1024)(128)(4,1)}), s8[4194304]{0:T(1024)(128)(4,1)S(1)}, s32[]{:S(2)}) async-start(s8[20971520]{0:T(1024)(128)(4,1)} %bitcast.301), calls=%async_computation.9 | async-start | bytes 8388608
  458.4 13.9 %slice-start.8 = ((s8[20971520]{0:T(1024)(128)(4,1)}), s8[4194304]{0:T(1024)(128)(4,1)S(1)}, s32[]{:S(2)}) async-start(s8[20971520]{0:T(1024)(128)(4,1)} %bitcast.301), calls=%async_computation.10 | async-start | bytes 8388608
  458.5 15.1 %slice-start.9 = ((s8[20971520]{0:T(1024)(128)(4,1)}), s8[4194304]{0:T(1024)(128)(4,1)S(1)}, s32[]{:S(2)}) async-start(s8[20971520]{0:T(1024)(128)(4,1)} %bitcast.301), calls=%async_computation.11 | async-start | bytes 8388608
  495.9 12.5 %slice-start.2 = ((s8[20971520]{0:T(1024)(128)(4,1)}), s8[4194304]{0:T(1024)(128)(4,1)S(1)}, s32[]{:S(2)}) async-start(s8[20971520]{0:T(1024)(128)(4,1)} %bitcast.299), calls=%async_computation.4 | async-start | bytes 8388608
  495.9 13.7 %slice-start.3 = ((s8[20971520]{0:T(1024)(128)(4,1)}), s8[4194304]{0:T(1024)(128)(4,1)S(1)}, s32[]{:S(2)}) async-start(s8[20971520]{0:T(1024)(128)(4,1)} %bitcast.299), calls=%async_computation.5 | async-start | bytes 8388608
  495.9 14.9 %slice-start.4 = ((s8[20971520]{0:T(1024)(128)(4,1)}), s8[4194304]{0:T(1024)(128)(4,1)S(1)}, s32[]{:S(2)}) async-start(s8[20971520]{0:T(1024)(128)(4,1)} %bitcast.299), calls=%async_computation.6 | async-start | bytes 8388608
  510.8 12.9 %copy-start.12 = (f32[4,5,512]{2,1,0:T(8,128)S(1)}, f32[4,5,512]{2,1,0:T(8,128)}, u32[]{:S(2)}) copy-start(f32[4,5,512]{2,1,0:T(8,128)} %copy-done.11) | copy-start | bytes 122884
  510.8 13.0 %copy-start.14 = (f32[4,5,512]{2,1,0:T(8,128)S(1)}, f32[4,5,512]{2,1,0:T(8,128)}, u32[]{:S(2)}) copy-start(f32[4,5,512]{2,1,0:T(8,128)} %copy-done.13) | copy-start | bytes 122884
  510.8 13.0 %copy-start.16 = (f32[4,5,512]{2,1,0:T(8,128)S(1)}, f32[4,5,512]{2,1,0:T(8,128)}, u32[]{:S(2)}) copy-start(f32[4,5,512]{2,1,0:T(8,128)} %copy-done.15) | copy-start | bytes 122884
  510.8 13.0 %copy-start.19 = (f32[4,5,512]{2,1,0:T(8,128)S(1)}, f32[4,5,512]{2,1,0:T(8,128)}, u32[]{:S(2)}) copy-start(f32[4,5,512]{2,1,0:T(8,128)} %fusion.14) | copy-start | bytes 122884
  510.8 13.0 %copy-start.20 = (f32[4,5,512]{2,1,0:T(8,128)S(1)}, f32[4,5,512]{2,1,0:T(8,128)}, u32[]{:S(2)}) copy-start(f32[4,5,512]{2,1,0:T(8,128)} %get-tuple-element.44) | copy-start | bytes 122884
  510.8 13.0 %copy-start.21 = (f32[4,5,512]{2,1,0:T(8,128)S(1)}, f32[4,5,512]{2,1,0:T(8,128)}, u32[]{:S(2)}) copy-start(f32[4,5,512]{2,1,0:T(8,128)} %get-tuple-element.45) | copy-start | bytes 122884
  (9 other events, 85.2 us)
Sparse Core Ops, SparseCore 0:
  8.9 17.9 all-gather.2
  29.6 343.7 all-gather.4
where the time goes:
time: 561 us; the launch traced here: 552 us
  waiting for transfers between devices  327 us (58%)
  matrix products  124 us (22%)
  other arithmetic  41.2 us (7%)
  local copies, waits for them, and re-layouts  25 us (4%)
  starting transfers between devices  20.3 us (4%)
  between operations  14.2 us (3%)
    all_gather x1, waiting for transfers between devices, on_device(): lax.all_gather(w_query, 'ctx', axis=0, tiled=True)  220 us
    ppermute x4, waiting for transfers between devices, shifted(): return lax.ppermute(block, axis, route)  105 us
    dot_general x5, matrix products, attend(): jnp.einsum('kgqp,pkd->kgqd', weights.astype(jnp.bfloat16), value_three, p...  60.2 us
    dot_general x5, matrix products, attend(): jnp.einsum('qkgd,pkd->kgqp', query_four, key_three, preferred_element_typ...  42.7 us
    reduce_sum x3, other arithmetic, attend(): weight_sum = weight_sum * rescale + jnp.sum(weights, axis=-1)  32.4 us
    dot_general x1, matrix products, on_device(): jnp.dot(normed, lax.all_gather(w_query, 'ctx', axis=0, tiled=True), prefe...  21.2 us
    ppermute x4, starting transfers between devices, shifted(): return lax.ppermute(block, axis, route)  20.3 us
  transfers between devices with their start and end apart: 6, of which 5 were waited for; matrix products, arithmetic and copies ran while one was open for 4% of the time, Pallas kernels for 0%

commit v1 on v0

v1 whole, which is shorter than its diff:
```python
import math

import jax
import jax.numpy as jnp
from jax import lax
from jax.experimental import pallas as pl
from jax.experimental.pallas import tpu as pltpu
from jax.sharding import PartitionSpec as P

HD = 128
TILE = 128
MAXDOC = 2048
KEYS = 512
QUERIES = 256
CHUNKS = 4
FAR = 1 << 30
MASKED = -1e30


epsilon = 1e-05
exp2_scale = math.log2(math.e) / HD**0.5


def rows_kernel(counts, distances, shapes, info, marks_smem, marks_ref, *refs):
    parts, kv_count, mask_width = counts
    tok_rows, shard_rows, source_rows = shapes
    n = len(distances)
    token_hbm = [refs[k * parts : (k + 1) * parts] for k in range(n)]
    w_hbm = refs[n * parts]
    kv_hbm = refs[n * parts + 1 :][:kv_count]
    out_hbm = refs[n * parts + 1 + kv_count :][:n]
    scratch = refs[n * parts + 1 + kv_count + n :]
    token_ref, w_ref, key_ref, value_ref, total_ref, query_ref, doc_full, acc_ref, max_ref, sum_ref, out_ref = scratch[:11]
    token_sem, w_sem, kv_sem, out_sem = scratch[11:]
    columns = w_ref.shape[1]
    heads = columns // HD
    depth = w_ref.shape[0]
    blocks = depth // source_rows
    halves = kv_hbm[0].shape[0]
    swap = info[1]
    chunk = depth // CHUNKS
    chunks_part = CHUNKS // parts
    doc_rows = tok_rows // TILE
    window_rows = halves * kv_count * shard_rows
    base = window_rows - kv_count * shard_rows

    def token_copy(ref, at, place, slot):
        target = pl.ds(pl.multiple_of(place * chunk, 128), chunk)
        return pltpu.make_async_copy(
            ref.at[:, at * chunk : (at + 1) * chunk], token_ref.at[slot, :, target], token_sem.at[slot, place]
        )

    def fetch_tokens(k):
        for part in range(parts):
            for at in range(chunks_part):
                token_copy(token_hbm[k][part], at, lax.bitwise_xor(info[2], part) * chunks_part + at, k % 2).start()

    def w_copy(at, place):
        target = pl.ds(pl.multiple_of(place * source_rows, 16), source_rows)
        return pltpu.make_async_copy(w_hbm.at[at], w_ref.at[target], w_sem.at[place])

    def kv_copy(ref, half, which, place):
        target = pl.ds(pl.multiple_of(KEYS + place * shard_rows, 16), shard_rows)
        return pltpu.make_async_copy(
            ref.at[half, which], (key_ref, value_ref)[which].at[target], kv_sem.at[place, which]
        )

    def out_copy(k, slot):
        return pltpu.make_async_copy(out_ref.at[slot], out_hbm[k], out_sem.at[slot])

    fetch_tokens(0)
    for at in range(blocks):
        w_copy(at, lax.bitwise_xor(swap, at)).start()
    for at in range(kv_count):
        for half in range(halves):
            for which in range(2):
                kv_copy(kv_hbm[at], half, which, half * kv_count + lax.bitwise_xor(swap, at)).start()
    key_ref[0:KEYS, :] = jnp.zeros((KEYS, HD), jnp.bfloat16)
    value_ref[0:KEYS, :] = jnp.zeros((KEYS, HD), jnp.bfloat16)

    stacked = heads * QUERIES
    subs = QUERIES // TILE

    def one_rows(k, carry):
        slot = lax.rem(k, 2)
        for ahead in range(1, n):

            @pl.when(k == ahead - 1)
            def _():
                fetch_tokens(ahead)

        for c in range(CHUNKS):
            token_copy(token_hbm[0][0], 0, c, slot).wait()

            @pl.when(k == 0)
            def _():
                for place in range(c * (blocks // CHUNKS), (c + 1) * (blocks // CHUNKS)):
                    w_copy(0, place).wait()

            piece = jnp.dot(
                token_ref[slot, :, c * chunk : (c + 1) * chunk],
                w_ref[c * chunk : (c + 1) * chunk, :],
                preferred_element_type=jnp.float32,
            )
            if c == 0:
                total_ref[...] = piece
            else:
                total_ref[...] += piece
        for tile in range(tok_rows // QUERIES):
            for head in range(heads):
                at = (tile * heads + head) * QUERIES
                query_ref[at : at + QUERIES, :] = total_ref[
                    tile * QUERIES : (tile + 1) * QUERIES, head * HD : (head + 1) * HD
                ].astype(jnp.bfloat16)

        @pl.when(k == 0)
        def _():
            for place in range(kv_count * halves):
                for which in range(2):
                    kv_copy(kv_hbm[0], 0, which, place).wait()

        @pl.when(k >= 2)
        def _():
            out_copy(0, slot).wait()

        distance = jnp.int32(distances[0])
        for other in range(1, n):
            distance = jnp.where(k == other, distances[other], distance)
        rows_first = base + lax.bitwise_xor(swap, distance) * tok_rows

        def one_tile(tile, carry):
            query = query_ref[pl.ds(pl.multiple_of(tile * stacked, stacked), stacked), :]
            row_first = rows_first + tile * QUERIES
            end = row_first + QUERIES
            for sub in range(subs):
                docs_row = marks_ref[k, pl.ds(tile * subs + sub, 1), :].astype(jnp.float32)
                doc_full[sub] = jnp.transpose(jnp.broadcast_to(docs_row, (TILE, TILE))).astype(jnp.int32)
            first_key = marks_smem[k, tile * subs, 0] - info[0]
            count = (end - first_key + KEYS - 1) // KEYS

            def one_block(back, carry):
                start = end - (back + 1) * KEYS
                at = pl.multiple_of(start + KEYS, TILE)
                keys = key_ref[pl.ds(at, KEYS), :]
                values = value_ref[pl.ds(at, KEYS), :]
                scores = lax.dot_general(query, keys, (((1,), (1,)), ((), ())), preferred_element_type=jnp.float32)
                key_tile = (info[0] + start) // TILE
                lane = lax.broadcasted_iota(jnp.int32, (TILE, TILE), 1)
                row = lax.broadcasted_iota(jnp.int32, (TILE, TILE), 0)
                masks = []
                for sub in range(subs):
                    causal = row + (row_first + sub * TILE - start)
                    docs = doc_full[sub] - (info[0] + start)
                    pieces = []
                    for m in range(KEYS // TILE):
                        column = lax.min(lax.max(key_tile + m, 0), mask_width - 1)
                        flat = (tile * subs + sub) * mask_width + column
                        shut = jnp.where(marks_smem[k, doc_rows + flat // TILE, lax.rem(flat, TILE)] == 1, 0, FAR)
                        pieces.append((lane <= causal - m * TILE) & (lane >= docs + (shut - m * TILE)))
                    masks.append(jnp.concatenate(pieces, axis=1))
                visible = jnp.concatenate(masks, axis=0)
                scores = jnp.where(visible[None], scores.reshape(heads, QUERIES, KEYS), MASKED).reshape(stacked, KEYS)
                old = max_ref[...]
                new = jnp.maximum(old, jnp.max(scores, axis=1, keepdims=True))
                alpha = jnp.exp2((old - new) * exp2_scale)
                shift = jnp.concatenate([new * exp2_scale] * (KEYS // HD), axis=1)
                weights = jnp.exp2(scores * exp2_scale - shift)
                max_ref[...] = new
                folded = weights[:, :HD]
                for m in range(1, KEYS // HD):
                    folded = folded + weights[:, m * HD : (m + 1) * HD]
                sum_ref[...] = sum_ref[...] * alpha + folded
                product = jnp.dot(weights.astype(jnp.bfloat16), values, preferred_element_type=jnp.float32)
                acc_ref[...] = acc_ref[...] * alpha + product
                return carry

            max_ref[...] = jnp.full(max_ref.shape, MASKED, jnp.float32)
            sum_ref[...] = jnp.zeros(sum_ref.shape, jnp.float32)
            acc_ref[...] = jnp.zeros(acc_ref.shape, jnp.float32)
            lax.fori_loop(0, count, one_block, 0)
            result = acc_ref[...] / jnp.sum(sum_ref[...], axis=1, keepdims=True)
            for head in range(heads):
                out_ref[slot, pl.ds(pl.multiple_of(tile * QUERIES, QUERIES), QUERIES), head * HD : (head + 1) * HD] = (
                    result[head * QUERIES : (head + 1) * QUERIES].astype(out_ref.dtype)
                )
            return carry

        lax.fori_loop(0, tok_rows // QUERIES, one_tile, 0)
        for at in range(n):

            @pl.when(k == at)
            def _():
                out_copy(at, at % 2).start()

        return carry

    lax.fori_loop(0, n, one_rows, 0)
    for k in range(max(n - 2, 0), n):
        out_copy(k, k % 2).wait()


def attend(info, marks, distances, token_parts, w_blocks, kv_parts, mask_width):
    n = len(distances)
    parts = len(token_parts[0])
    rows = token_parts[0][0].shape[0]
    source_rows, columns = w_blocks.shape[1:]
    depth = w_blocks.shape[0] * source_rows
    heads = columns // HD
    shard_rows = kv_parts[0].shape[2]
    shards = len(kv_parts) * kv_parts[0].shape[0]
    vmem = pl.BlockSpec(memory_space=pltpu.VMEM)
    smem = pl.BlockSpec(memory_space=pltpu.SMEM)
    leave = pl.BlockSpec(memory_space=pl.ANY)
    arrays = [part for block in token_parts for part in block] + [w_blocks] + list(kv_parts)
    counts = (parts, len(kv_parts), mask_width)
    tile_rows = heads * QUERIES

    def kernel(*refs):
        rows_kernel(counts, distances, (rows, shard_rows, source_rows), *refs)

    return pl.pallas_call(
        kernel,
        out_shape=[jax.ShapeDtypeStruct((rows, columns), jnp.bfloat16)] * n,
        in_specs=[smem, smem, vmem] + [leave] * len(arrays),
        out_specs=[leave] * n,
        scratch_shapes=[
            pltpu.VMEM((2, rows, depth), jnp.bfloat16),
            pltpu.VMEM((depth, columns), jnp.bfloat16),
            pltpu.VMEM((KEYS + shards * shard_rows, HD), jnp.bfloat16),
            pltpu.VMEM((KEYS + shards * shard_rows, HD), jnp.bfloat16),
            pltpu.VMEM((rows, columns), jnp.float32),
            pltpu.VMEM((rows * heads, HD), jnp.bfloat16),
            pltpu.VMEM((QUERIES // TILE, TILE, TILE), jnp.int32),
            pltpu.VMEM((tile_rows, HD), jnp.float32),
            pltpu.VMEM((tile_rows, HD), jnp.float32),
            pltpu.VMEM((tile_rows, HD), jnp.float32),
            pltpu.VMEM((2, rows, columns), jnp.bfloat16),
            pltpu.SemaphoreType.DMA((2, CHUNKS)),
            pltpu.SemaphoreType.DMA((w_blocks.shape[0],)),
            pltpu.SemaphoreType.DMA((shards, 2)),
            pltpu.SemaphoreType.DMA((2,)),
        ],
        compiler_params=pltpu.CompilerParams(vmem_limit_bytes=60 << 20),
        cost_estimate=pl.CostEstimate(
            flops=n * (2 * rows * depth * columns + 4 * rows * columns * 1024),
            bytes_accessed=2 * (n * rows * depth + depth * columns + shards * 2 * shard_rows * HD + n * rows * columns),
            transcendentals=n * rows * heads * 1024,
        ),
    )(info, marks, marks, *arrays)


def marks_of(doc_start, tile_mask):
    return jnp.concatenate([doc_start.reshape(-1, TILE), tile_mask.reshape(-1, TILE)])


def planar(tokens, norm_gain, w_query, cache_keys, cache_values, doc_start, tile_mask, group):
    devices = lax.axis_size("ctx")
    index = lax.axis_index("ctx")
    core = lax.axis_index("tp")
    place = lax.rem(index, group)
    tok_rows, width = tokens.shape
    kv_width = cache_keys.shape[1] // group
    q_width = w_query.shape[1] // group
    rows = group * tok_rows
    lines = [[first + k for first in range(0, devices, group)] for k in range(group)]
    far = range(1, group)

    def swapped(block, distance):
        return lax.ppermute(block, "ctx", [(i, i ^ distance) for i in range(devices)])

    def other_core(block):
        return lax.ppermute(block, "tp", [(0, 1), (1, 0)])

    def columns_for(array, distance, first, size, of, axis):
        at = lax.bitwise_xor(place, distance) * of + first
        return lax.dynamic_slice_in_dim(array, at, size, axis)

    def after(values, *earlier):
        flat = lax.optimization_barrier((tuple(values), tuple(earlier)))
        return list(flat[0])

    kv_own = jnp.stack([cache_keys, cache_values])
    first_columns = (q_width // HD + 1) // 2 * HD
    cuts = ((0, first_columns), (first_columns, q_width))

    marks_own = marks_of(doc_start, tile_mask)
    w_first = [columns_for(w_query, d, cuts[0][0], cuts[0][1] - cuts[0][0], q_width, 1) for d in range(group)]
    marks = [marks_own] + [swapped(marks_own, d) for d in far]
    w_first = w_first[:1] + [swapped(w_first[d], d) for d in far]
    kv_before = lax.ppermute(kv_own, "ctx", [(i, i + group) for i in range(devices - group)])

    float_tokens = tokens.astype(jnp.float32)
    squares = jnp.sum(float_tokens * float_tokens, axis=-1)
    squares = squares + other_core(squares)
    inverse = lax.rsqrt(squares / (2 * width) + epsilon)
    gain = lax.dynamic_slice_in_dim(norm_gain, core * width, width, 0)
    normed = (float_tokens * inverse[:, None] * gain).astype(jnp.bfloat16)

    w_stack = jnp.stack(w_first)
    w_chunks = [lax.all_gather(w_stack, "ctx", axis=0, tiled=True, axis_index_groups=lines)]
    w_second = [columns_for(w_query, d, cuts[1][0], cuts[1][1] - cuts[1][0], q_width, 1) for d in range(group)]
    w_second = after(w_second, w_stack, *marks)
    w_second = w_second[:1] + [swapped(w_second[d], d) for d in far]
    w_stack = jnp.stack(w_second)
    (w_after,) = after([w_stack], w_chunks[0])
    w_chunks.append(lax.all_gather(w_after, "ctx", axis=0, tiled=True, axis_index_groups=lines))

    kv_two = jnp.stack([kv_before, kv_own])
    kv_cut = after([columns_for(kv_two, d, 0, kv_width, kv_width, 3) for d in range(group)], w_stack)
    (normed,) = after([normed], w_stack, kv_before)
    kv_parts = kv_cut[:1] + [swapped(kv_cut[d], d) for d in far]
    from_x, from_y = swapped(normed, 1), swapped(normed, 2)
    mine_other = other_core(normed)

    half = width // 2
    relay_y, relay_x = after([from_y[:, :half], from_x[:, half:]], *kv_parts)
    corner_a, corner_b = swapped(relay_y, 1), swapped(relay_x, 2)
    corner = jnp.concatenate([corner_a, corner_b], axis=1)
    mine = [normed, from_x, from_y, corner]
    token_parts = [[normed, mine_other]] + [[mine[d], other_core(mine[d])] for d in far]

    info = jnp.stack([(index // group - 1) * rows, place, core]).astype(jnp.int32)
    width_mask = tile_mask.shape[1]

    def call(distances, chunk, *earlier):
        chosen = [token_parts[d] for d in distances]
        (start,) = after([info], *earlier)
        picked = jnp.stack([marks[d] for d in distances])
        return attend(start, picked, distances, chosen, chunk, kv_parts, width_mask)

    outs = dict(zip((3, 2, 1, 0), call((3, 2, 1, 0), w_chunks[0])))
    pieces = {(d, 0): swapped(out, d) if d else out for d, out in outs.items()}
    outs = dict(zip((3, 2, 1), call((3, 2, 1), w_chunks[1], outs[0])))
    pieces.update({(d, 1): swapped(out, d) for d, out in outs.items()})
    pieces[0, 1] = call((0,), w_chunks[1], outs[1])[0]
    return joined(info, pieces, q_width, [low for low, _ in cuts], group * q_width)


def joined(info, pieces, q_width, lows, columns):
    keys = sorted(pieces)
    rows = pieces[keys[0]].shape[0]
    leave = pl.BlockSpec(memory_space=pl.ANY)

    def kernel(info_ref, *refs):
        out_hbm, sem = refs[-2:]

        def copy(k):
            distance, chunk = keys[k]
            at = pl.multiple_of(lax.bitwise_xor(info_ref[1], distance) * q_width + lows[chunk], HD)
            target = out_hbm.at[:, pl.ds(at, refs[k].shape[1])]
            return pltpu.make_async_copy(refs[k], target, sem.at[k])

        for k in range(len(keys)):
            copy(k).start()
        for k in range(len(keys)):
            copy(k).wait()

    return pl.pallas_call(
        kernel,
        out_shape=jax.ShapeDtypeStruct((rows, columns), jnp.bfloat16),
        in_specs=[pl.BlockSpec(memory_space=pltpu.SMEM)] + [leave] * len(keys),
        out_specs=leave,
        scratch_shapes=[pltpu.SemaphoreType.DMA((len(keys),))],
        cost_estimate=pl.CostEstimate(flops=0, bytes_accessed=4 * rows * columns, transcendentals=0),
    )(info, *[pieces[key] for key in keys])


def plain(tokens, norm_gain, w_query, cache_keys, cache_values, doc_start, tile_mask):
    devices = lax.axis_size("ctx")
    index = lax.axis_index("ctx")
    tok_rows = tokens.shape[0]
    float_tokens = lax.all_gather(tokens, "tp", axis=1, tiled=True).astype(jnp.float32)
    inverse = lax.rsqrt(jnp.mean(float_tokens * float_tokens, axis=-1, keepdims=True) + epsilon)
    normed = (float_tokens * inverse * norm_gain).astype(jnp.bfloat16)
    kv_heads = cache_keys.shape[1] // HD
    q_width = w_query.shape[1] // kv_heads
    w_blocks = lax.all_gather(w_query, "ctx", axis=0)
    reach = (MAXDOC + tok_rows - 2) // tok_rows
    kv_own = jnp.stack([cache_keys, cache_values])
    shards = [
        lax.ppermute(kv_own, "ctx", [(i, i + distance) for i in range(devices - distance)])
        for distance in range(reach, 0, -1)
    ]
    kv_window = jnp.stack(shards + [kv_own])
    info = jnp.stack([(index - reach) * tok_rows, jnp.int32(0), jnp.int32(0)]).astype(jnp.int32)
    marks = marks_of(doc_start, tile_mask)[None]
    outs = [
        attend(
            info,
            marks,
            (0,),
            [[normed]],
            w_blocks[:, :, head * q_width : (head + 1) * q_width],
            [kv_window[:, :, :, head * HD : (head + 1) * HD]],
            tile_mask.shape[1],
        )[0]
        for head in range(kv_heads)
    ]
    return outs[0] if kv_heads == 1 else jnp.concatenate(outs, axis=1)


def on_device(*arrays):
    kv_heads = arrays[3].shape[1] // HD
    group = 4
    rows = group * arrays[0].shape[0]
    if kv_heads == group and lax.axis_size("ctx") % group == 0 and lax.axis_size("tp") == 2 and rows >= MAXDOC - 1:
        return planar(*arrays, group)
    return plain(*arrays)


def solution(mesh):
    return jax.shard_map(
        on_device,
        mesh=mesh,
        in_specs=(
            P("ctx", "tp"),
            P(),
            P("ctx", "tp"),
            P("ctx", "tp"),
            P("ctx", "tp"),
            P("ctx"),
            P("ctx", None),
        ),
        out_specs=P("ctx", "tp"),
        check_vma=False,
    )
```

time: 561 us -> 386 us (0.69); the launches traced: 552 us -> 384 us
  waiting for transfers between devices: 327 us -> 152 us
  Pallas kernels: 0 us -> 157 us
  matrix products: 124 us -> 0 us
  other arithmetic: 41.2 us -> 13.8 us
  starting transfers between devices: 20.3 us -> 33.9 us
  local copies, waits for them, and re-layouts: 25 us -> 14.3 us
    all_gather x2, waiting for transfers between devices: 220 us -> 22.9 us  [the longest x1 22.9 us: planar(): lax.all_gather(w_after, 'ctx', axis=0, tiled=True, axis_index_groups=lines)]
    pallas_call x0 -> x4, Pallas kernels: none -> 157 us  [the longest x1 81.2 us: joined(): pl.pallas_call(kernel, out_shape=jax.ShapeDtypeStruct((rows, columns), jn...]
    dot_general x11 -> x0, matrix products: 124 us -> none  [the longest x5 60.2 us: attend(): jnp.einsum('kgqp,pkd->kgqd', weights.astype(jnp.bfloat16), value_three, p...]
    reduce_sum x4 -> x1, other arithmetic: 36 us -> 0.59 us  [planar(): squares = jnp.sum(float_tokens * float_tokens, axis=-1)]
    ppermute x4 -> x28, waiting for transfers between devices: 105 us -> 129 us  [the longest x22 99.4 us: swapped(): lax.ppermute(block, 'ctx', [(i, i ^ distance) for i in range(devices)])]
    ppermute x4 -> x28, starting transfers between devices: 20.3 us -> 33.9 us  [the longest x22 28.7 us: swapped(): lax.ppermute(block, 'ctx', [(i, i ^ distance) for i in range(devices)])]
    another operation x1 -> x7, other arithmetic: 0.1 us -> 10.4 us  [the longest x2 5.06 us: planar(): kv_two = jnp.stack([kv_before, kv_own])]
    convert_element_type x2 -> x0, local copies, waits for them, and re-layouts: 5.76 us -> none  [the longest x1 2.99 us: on_device(): queries = jnp.dot(normed, lax.all_gather(w_query, 'ctx', axis=0, tiled=Tr...]
  transfers between devices with their start and end apart: 6 -> 30, of which waited for: 5 -> 13; matrix products, arithmetic and copies ran while one was open for 4% -> 6% of each run, Pallas kernels for 0% -> 20%
where the time goes in v1:
time: 386 us; the launch traced here: 384 us
  Pallas kernels  157 us (41%)
  waiting for transfers between devices  152 us (39%)
  starting transfers between devices  33.9 us (9%)
  local copies, waits for them, and re-layouts  14.3 us (4%)
  other arithmetic  13.8 us (4%)
  between operations  13.7 us (4%)
    ppermute x22, waiting for transfers between devices, swapped(): lax.ppermute(block, 'ctx', [(i, i ^ distance) for i in range(devices)])  99.4 us
    pallas_call x1, Pallas kernels, joined(): pl.pallas_call(kernel, out_shape=jax.ShapeDtypeStruct((rows, columns), jn...  81.2 us
    pallas_call x3, Pallas kernels, attend(): pl.pallas_call(kernel, out_shape=[jax.ShapeDtypeStruct((rows, columns), j...  75.3 us
    ppermute x22, starting transfers between devices, swapped(): lax.ppermute(block, 'ctx', [(i, i ^ distance) for i in range(devices)])  28.7 us
    ppermute x1, waiting for transfers between devices, planar(): lax.ppermute(kv_own, 'ctx', [(i, i + group) for i in range(devices - grou...  26.3 us
    all_gather x1, waiting for transfers between devices, planar(): lax.all_gather(w_after, 'ctx', axis=0, tiled=True, axis_index_groups=lines)  22.9 us
  transfers between devices with their start and end apart: 30, of which 13 were waited for; matrix products, arithmetic and copies ran while one was open for 6% of the time, Pallas kernels for 20%

profile of v1, /device:TPU:0, one launch (start us, length us, event | category | flops | bytes accessed | tf_op | source)
XLA Modules:
  0.0 384.4 jit_solution(1341994353229577142)
XLA Ops:
  6.5 1.5 dynamic-slice_bitcast_fusion
  8.0 3.0 collective-permute-start.5
  11.0 1.4 collective-permute-start.6
  14.0 2.9 collective-permute-start
  17.4 4.9 %collective-permute-done.5 = bf16[320,384]{1,0:T(8,128)(2,1)S(1)} collective-permute-done((bf16[320,384]{1,0:T(8,128)(2,1)S(1)}, bf16[320,384]{1,0:T(8,128)(2,1)S(1)}, u32[]{:S(2)}, u32[]{:S(2)}) %collective-permute-start.5) | collective-permute-done | bytes 245792 | tf_op jit(solution)/shard_map/ppermute | solution.py:269
  22.3 1.7 collective-permute-start.2
  24.8 2.5 pad_maximum_fusion.1
  27.4 2.5 fusion.8
  29.9 4.6 %collective-permute-start.10 = (bf16[2,512,512]{2,1,0:T(8,128)(2,1)}, bf16[2,512,512]{2,1,0:T(8,128)(2,1)}, u32[]{:S(2)}, u32[]{:S(2)}) collective-permute-start(bf16[2,512,512]{2,1,0:T(8,128)(2,1)} %get-tuple-element.60), channel_id=1, source_target_pairs={{0,8},{2,10},{4,12},{6,14},{8,16},{10,18},{12,20},{14,22},{16,24},... | collective-permute-start | bytes 3145736 | tf_op jit(solution)/shard_map/ppermute | solution.py:290
  37.9 1.5 collective-permute-start.8
  40.3 2.2 fusion.2.refs_9_.refs_3_
  43.8 3.0 collective-permute-done.8
  48.8 26.3 %collective-permute-done.10 = bf16[2,512,512]{2,1,0:T(8,128)(2,1)} collective-permute-done((bf16[2,512,512]{2,1,0:T(8,128)(2,1)}, bf16[2,512,512]{2,1,0:T(8,128)(2,1)}, u32[]{:S(2)}, u32[]{:S(2)}) %collective-permute-start.10) | collective-permute-done | bytes 1048608 | tf_op jit(solution)/shard_map/ppermute | solution.py:290
  77.3 2.5 fusion.3
  81.8 1.6 collective-permute-start.15
  83.3 51.1 %collective-permute-done.11.refs_5_ = bf16[512,2560]{1,0:T(8,128)(2,1)} collective-permute-done((bf16[512,2560]{1,0:T(8,128)(2,1)}, bf16[512,2560]{1,0:T(8,128)(2,1)}, u32[]{:S(2)}, u32[]{:S(2)}) %collective-permute-start.11) | collective-permute-done | bytes 2621472 | tf_op jit(solution)/shard_map/ppermute | solution.py:269
  134.4 1.4 slice.8
  136.7 2.5 slice.9
  139.1 5.8 %collective-permute-done.13.refs_13_.refs_11_.refs_7_ = bf16[2,2,512,128]{3,2,1,0:T(8,128)(2,1)S(1)} collective-permute-done((bf16[2,2,512,128]{3,2,1,0:T(8,128)(2,1)S(1)}, bf16[2,2,512,128]{3,2,1,0:T(8,128)(2,1)S(1)}, u32[]{:S(2)}, u32[]{:S(2)}) %collective-permute-start.13) | collective-permute-done | bytes 524320 | tf_op jit(solution)/shard_map/ppermute | solution.py:269
  145.8 10.3 %collective-permute-done.15.refs_15_.refs_13_.refs_9_ = bf16[2,2,512,128]{3,2,1,0:T(8,128)(2,1)} collective-permute-done((bf16[2,2,512,128]{3,2,1,0:T(8,128)(2,1)S(1)}, bf16[2,2,512,128]{3,2,1,0:T(8,128)(2,1)}, u32[]{:S(2)}, u32[]{:S(2)}) %collective-permute-start.15) | collective-permute-done | bytes 524320 | tf_op jit(solution)/shard_map/ppermute | solution.py:269
  156.3 2.5 collective-permute-start.17
  159.3 19.3 %collective-permute-done.16 = bf16[512,1280]{1,0:T(8,128)(2,1)S(1)} collective-permute-done((bf16[512,1280]{1,0:T(8,128)(2,1)S(1)}, bf16[512,1280]{1,0:T(8,128)(2,1)S(1)}, u32[]{:S(2)}, u32[]{:S(2)}) %collective-permute-start.16) | collective-permute-done | bytes 1310752 | tf_op jit(solution)/shard_map/ppermute | solution.py:269
  179.9 2.6 constant_dynamic-update-slice_fusion.refs_3_
  184.3 3.4 collective-permute-done.18.refs_4_
  187.7 37.4 %shard_map.73 = (bf16[512,384]{1,0:T(8,128)(2,1)}, bf16[512,384]{1,0:T(8,128)(2,1)}, bf16[512,384]{1,0:T(8,128)(2,1)}, bf16[512,384]{1,0:T(8,128)(2,1)}) custom-call(s32[3]{0:T(128)} %pad_add_fusion.3.refs_0_.info_ref, s32[4,6,128]{2,1,0:T(8,128)} %pad_add_fusion.refs_1_.refs_2_, s32[4,6,128]{2,1,0:T(8,128)} %pad_add_fusion.refs_1_.refs_2_, ...), custom_call_target="tpu_custom_call" | custom-call | flops 11274289152 | bytes 28573696 | tf_op jit(solution)/shard_map/pallas_call | solution.py:221
  226.8 1.8 collective-permute-start.26
  228.7 22.9 %all-gather.5.cloned.1.call-done.refs_9_.refs_5_ = bf16[16,320,256]{2,1,0:T(8,128)(2,1)} async-done(((bf16[4,320,256]{2,1,0:T(8,128)(2,1)}), bf16[16,320,256]{2,1,0:T(8,128)(2,1)}) %all-gather.5.cloned.1.call-update) | async-done | bytes 2621456 | tf_op jit(solution)/shard_map/all_gather | solution.py:306
  251.6 28.4 %shard_map.74 = (bf16[512,256]{1,0:T(8,128)(2,1)}, bf16[512,256]{1,0:T(8,128)(2,1)}, bf16[512,256]{1,0:T(8,128)(2,1)}) custom-call(s32[3]{0:T(128)} %pad_add_fusion.3.refs_0_.info_ref, s32[3,6,128]{2,1,0:T(8,128)} %pad_add_fusion.1.refs_1_.refs_2_, s32[3,6,128]{2,1,0:T(8,128)} %pad_add_fusion.1.refs_1_.refs_2_, ...), custom_call_target="tpu_custom_call" | custom-call | flops 5637144576 | bytes 21233664 | tf_op jit(solution)/shard_map/pallas_call | solution.py:221
  280.2 3.4 collective-permute-start.27
  283.6 9.5 %shard_map.75.refs_1_ = bf16[512,256]{1,0:T(8,128)(2,1)} custom-call(s32[3]{0:T(128)} %pad_add_fusion.3.refs_0_.info_ref, s32[1,6,128]{2,1,0:T(8,128)} %copy-done.14, s32[1,6,128]{2,1,0:T(8,128)} %copy-done.14, bf16[512,2560]{1,0:T(8,128)(2,1)} %fusion.2.refs_9_.refs_3_, bf16[512,2560]{1,0:T(8,128)(2,1)} %collective-permute-done.21.refs_10_.refs_4_, ...), custom_call_target="tpu_custom_call" | custom-call | flops 1879048192 | bytes 10223616 | tf_op jit(solution)/shard_map/pallas_call | solution.py:221
  293.1 1.7 collective-permute-done.25.refs_5_
  296.3 81.2 %shard_map.76 = bf16[512,2560]{1,0:T(8,128)(2,1)} custom-call(s32[3]{0:T(128)} %pad_add_fusion.3.refs_0_.info_ref, bf16[512,384]{1,0:T(8,128)(2,1)} %get-tuple-element.37.refs_0_, bf16[512,256]{1,0:T(8,128)(2,1)} %shard_map.75.refs_1_, bf16[512,384]{1,0:T(8,128)(2,1)} %copy-done.5, bf16[512,256]{1,0:T(8,128)(2,1)} %copy-done.8, bf16[512,384]{1,0:T(8,128)(2,1)} %copy-done.6, ...), custom_call_target="tpu_custom_call" | custom-call | bytes 5242880 | tf_op jit(solution)/shard_map/pallas_call | solution.py:358
  (85 shorter events, 23.4 us)
Async XLA Ops:
  6.5 173.3 %all-gather.3.cloned.1.call-start = ((), (), s32[]{:S(2)}) async-start(), calls=%async_computation | async-start | bytes 4915200 | tf_op jit(solution)/shard_map/all_gather | solution.py:300
  8.0 14.3 %collective-permute-start.5 = (bf16[320,384]{1,0:T(8,128)(2,1)S(1)}, bf16[320,384]{1,0:T(8,128)(2,1)S(1)}, u32[]{:S(2)}, u32[]{:S(2)}) collective-permute-start(bf16[320,384]{1,0:T(8,128)(2,1)S(1)} %get-tuple-element.54), channel_id=1, source_target_pairs={{0,4},{2,6},{4,0},{6,2},{8,12},{10,14},{12,8},{14,10},{16,20},{18,... | collective-permute-start | bytes 737288 | tf_op jit(solution)/shard_map/ppermute | solution.py:269
  11.0 13.0 %collective-permute-start.6 = (bf16[320,384]{1,0:T(8,128)(2,1)S(1)}, bf16[320,384]{1,0:T(8,128)(2,1)S(1)}, u32[]{:S(2)}, u32[]{:S(2)}) collective-permute-start(bf16[320,384]{1,0:T(8,128)(2,1)S(1)} %get-tuple-element.53), channel_id=1, source_target_pairs={{0,6},{2,4},{4,2},{6,0},{8,14},{10,12},{12,10},{14,8},{16,22},{18,... | collective-permute-start | bytes 737288 | tf_op jit(solution)/shard_map/ppermute | solution.py:269
  12.5 11.6 %collective-permute-start.4 = (bf16[320,384]{1,0:T(8,128)(2,1)S(1)}, bf16[320,384]{1,0:T(8,128)(2,1)S(1)}, u32[]{:S(2)}, u32[]{:S(2)}) collective-permute-start(bf16[320,384]{1,0:T(8,128)(2,1)S(1)} %get-tuple-element.52), channel_id=1, source_target_pairs={{0,2},{2,0},{4,6},{6,4},{8,10},{10,8},{12,14},{14,12},{16,18},{18,... | collective-permute-start | bytes 737288 | tf_op jit(solution)/shard_map/ppermute | solution.py:269
  14.0 169.6 %copy-start.14 = (s32[1,6,128]{2,1,0:T(8,128)}, s32[1,6,128]{2,1,0:T(8,128)S(1)}, u32[]{:S(2)}) copy-start(s32[1,6,128]{2,1,0:T(8,128)S(1)} %get-tuple-element.62.refs_1_.refs_2_) | copy-start | bytes 9220
  14.0 22.7 %collective-permute-start = (s32[6,128]{1,0:T(8,128)S(1)}, s32[6,128]{1,0:T(8,128)S(1)}, u32[]{:S(2)}, u32[]{:S(2)}) collective-permute-start(s32[6,128]{1,0:T(8,128)S(1)} %get-tuple-element.61), channel_id=1, source_target_pairs={{0,6},{2,4},{4,2},{6,0},{8,14},{10,12},{12,10},{14,8},{16,22},{18,... | collective-permute-start | bytes 9224 | tf_op jit(solution)/shard_map/ppermute | solution.py:269
  16.9 19.8 %collective-permute-start.1 = (s32[6,128]{1,0:T(8,128)S(1)}, s32[6,128]{1,0:T(8,128)S(1)}, u32[]{:S(2)}, u32[]{:S(2)}) collective-permute-start(s32[6,128]{1,0:T(8,128)S(1)} %get-tuple-element.61), channel_id=1, source_target_pairs={{0,4},{2,6},{4,0},{6,2},{8,12},{10,14},{12,8},{14,10},{16,20},{18,... | collective-permute-start | bytes 9224 | tf_op jit(solution)/shard_map/ppermute | solution.py:269
  22.3 14.4 %collective-permute-start.2 = (s32[6,128]{1,0:T(8,128)S(1)}, s32[6,128]{1,0:T(8,128)S(1)}, u32[]{:S(2)}, u32[]{:S(2)}) collective-permute-start(s32[6,128]{1,0:T(8,128)S(1)} %get-tuple-element.61), channel_id=1, source_target_pairs={{0,2},{2,0},{4,6},{6,4},{8,10},{10,8},{12,14},{14,12},{16,18},{18,... | collective-permute-start | bytes 9224 | tf_op jit(solution)/shard_map/ppermute | solution.py:269
  27.4 224.2 %all-gather.5.cloned.1.call-start = ((), (), s32[]{:S(2)}) async-start(), calls=%async_computation.1 | async-start | bytes 3276800 | tf_op jit(solution)/shard_map/all_gather | solution.py:306
  29.9 45.2 %collective-permute-start.10 = (bf16[2,512,512]{2,1,0:T(8,128)(2,1)}, bf16[2,512,512]{2,1,0:T(8,128)(2,1)}, u32[]{:S(2)}, u32[]{:S(2)}) collective-permute-start(bf16[2,512,512]{2,1,0:T(8,128)(2,1)} %get-tuple-element.60), channel_id=1, source_target_pairs={{0,8},{2,10},{4,12},{6,14},{8,16},{10,18},{12,20},{14,22},{16,24},... | collective-permute-start | bytes 3145736 | tf_op jit(solution)/shard_map/ppermute | solution.py:290
  35.1 1.5 collective-permute-start.3
  36.7 7.1 %collective-permute-start.7 = (bf16[320,256]{1,0:T(8,128)(2,1)S(1)}, bf16[320,256]{1,0:T(8,128)(2,1)S(1)}, u32[]{:S(2)}, u32[]{:S(2)}) collective-permute-start(bf16[320,256]{1,0:T(8,128)(2,1)S(1)} %get-tuple-element.27), channel_id=1, source_target_pairs={{0,2},{2,0},{4,6},{6,4},{8,10},{10,8},{12,14},{14,12},{16,18},{18,... | collective-permute-start | bytes 491528 | tf_op jit(solution)/shard_map/ppermute | solution.py:269
  37.9 8.8 %collective-permute-start.8 = (bf16[320,256]{1,0:T(8,128)(2,1)S(1)}, bf16[320,256]{1,0:T(8,128)(2,1)S(1)}, u32[]{:S(2)}, u32[]{:S(2)}) collective-permute-start(bf16[320,256]{1,0:T(8,128)(2,1)S(1)} %get-tuple-element.28), channel_id=1, source_target_pairs={{0,4},{2,6},{4,0},{6,2},{8,12},{10,14},{12,8},{14,10},{16,20},{18,... | collective-permute-start | bytes 491528 | tf_op jit(solution)/shard_map/ppermute | solution.py:269
  39.4 8.4 %collective-permute-start.9 = (bf16[320,256]{1,0:T(8,128)(2,1)S(1)}, bf16[320,256]{1,0:T(8,128)(2,1)S(1)}, u32[]{:S(2)}, u32[]{:S(2)}) collective-permute-start(bf16[320,256]{1,0:T(8,128)(2,1)S(1)} %get-tuple-element.29), channel_id=1, source_target_pairs={{0,6},{2,4},{4,2},{6,0},{8,14},{10,12},{12,10},{14,8},{16,22},{18,... | collective-permute-start | bytes 491528 | tf_op jit(solution)/shard_map/ppermute | solution.py:269
  75.2 59.2 %collective-permute-start.11 = (bf16[512,2560]{1,0:T(8,128)(2,1)}, bf16[512,2560]{1,0:T(8,128)(2,1)}, u32[]{:S(2)}, u32[]{:S(2)}) collective-permute-start(bf16[512,2560]{1,0:T(8,128)(2,1)} %fusion.2.refs_9_.refs_3_), channel_id=1, source_target_pairs={{0,4},{2,6},{4,0},{6,2},{8,12},{10,14},{12,8},{14,10},{16,20},{18,... | collective-permute-start | bytes 7864328 | tf_op jit(solution)/shard_map/ppermute | solution.py:269
  76.6 60.1 %collective-permute-start.12 = (bf16[512,2560]{1,0:T(8,128)(2,1)}, bf16[512,2560]{1,0:T(8,128)(2,1)}, u32[]{:S(2)}, u32[]{:S(2)}) collective-permute-start(bf16[512,2560]{1,0:T(8,128)(2,1)} %fusion.2.refs_9_.refs_3_), channel_id=1, source_target_pairs={{0,2},{2,0},{4,6},{6,4},{8,10},{10,8},{12,14},{14,12},{16,18},{18,... | collective-permute-start | bytes 7864328 | tf_op jit(solution)/shard_map/ppermute | solution.py:269
  79.8 79.0 %copy-start.1 = (bf16[512,2560]{1,0:T(8,128)(2,1)S(1)}, bf16[512,2560]{1,0:T(8,128)(2,1)}, u32[]{:S(2)}) copy-start(bf16[512,2560]{1,0:T(8,128)(2,1)} %fusion.2.refs_9_.refs_3_) | copy-start | bytes 7864324
  79.8 65.1 %collective-permute-start.13 = (bf16[2,2,512,128]{3,2,1,0:T(8,128)(2,1)S(1)}, bf16[2,2,512,128]{3,2,1,0:T(8,128)(2,1)S(1)}, u32[]{:S(2)}, u32[]{:S(2)}) collective-permute-start(bf16[2,2,512,128]{3,2,1,0:T(8,128)(2,1)S(1)} %get-tuple-element.32), channel_id=1, source_target_pairs={{0,2},{2,0},{4,6},{6,4},{8,10},{10,8},{12,14},{14,12},{16,18},{18,... | collective-permute-start | bytes 1572872 | tf_op jit(solution)/shard_map/ppermute | solution.py:269
  81.1 63.8 %collective-permute-start.14 = (bf16[2,2,512,128]{3,2,1,0:T(8,128)(2,1)S(1)}, bf16[2,2,512,128]{3,2,1,0:T(8,128)(2,1)S(1)}, u32[]{:S(2)}, u32[]{:S(2)}) collective-permute-start(bf16[2,2,512,128]{3,2,1,0:T(8,128)(2,1)S(1)} %get-tuple-element.33), channel_id=1, source_target_pairs={{0,4},{2,6},{4,0},{6,2},{8,12},{10,14},{12,8},{14,10},{16,20},{18,... | collective-permute-start | bytes 1572872 | tf_op jit(solution)/shard_map/ppermute | solution.py:269
  81.8 74.3 %collective-permute-start.15 = (bf16[2,2,512,128]{3,2,1,0:T(8,128)(2,1)S(1)}, bf16[2,2,512,128]{3,2,1,0:T(8,128)(2,1)}, u32[]{:S(2)}, u32[]{:S(2)}) collective-permute-start(bf16[2,2,512,128]{3,2,1,0:T(8,128)(2,1)S(1)} %get-tuple-element.34), channel_id=1, source_target_pairs={{0,6},{2,4},{4,2},{6,0},{8,14},{10,12},{12,10},{14,8},{16,22},{18,... | collective-permute-start | bytes 1572872 | tf_op jit(solution)/shard_map/ppermute | solution.py:269
  156.1 22.6 %collective-permute-start.16 = (bf16[512,1280]{1,0:T(8,128)(2,1)S(1)}, bf16[512,1280]{1,0:T(8,128)(2,1)S(1)}, u32[]{:S(2)}, u32[]{:S(2)}) collective-permute-start(bf16[512,1280]{1,0:T(8,128)(2,1)S(1)} %slice.8), channel_id=1, source_target_pairs={{0,2},{2,0},{4,6},{6,4},{8,10},{10,8},{12,14},{14,12},{16,18},{18,... | collective-permute-start | bytes 3932168 | tf_op jit(solution)/shard_map/ppermute | solution.py:269
  156.3 23.6 %collective-permute-start.17 = (bf16[512,1280]{1,0:T(8,128)(2,1)}, bf16[512,1280]{1,0:T(8,128)(2,1)}, u32[]{:S(2)}, u32[]{:S(2)}) collective-permute-start(bf16[512,1280]{1,0:T(8,128)(2,1)} %slice.9), channel_id=1, source_target_pairs={{0,4},{2,6},{4,0},{6,2},{8,12},{10,14},{12,8},{14,10},{16,20},{18,... | collective-permute-start | bytes 3932168 | tf_op jit(solution)/shard_map/ppermute | solution.py:269
  158.8 25.5 %collective-permute-start.21 = (bf16[512,2560]{1,0:T(8,128)(2,1)S(1)}, bf16[512,2560]{1,0:T(8,128)(2,1)}, u32[]{:S(2)}, u32[]{:S(2)}) collective-permute-start(bf16[512,2560]{1,0:T(8,128)(2,1)S(1)} %copy-done.1), channel_id=1, source_target_pairs={{0,1},{1,0},{2,3},{3,2},{4,5},{5,4},{6,7},{7,6},{8,9},{9,8},{10,11... | collective-permute-start | bytes 7864328 | tf_op jit(solution)/shard_map/ppermute | solution.py:272
  158.8 25.5 %collective-permute-start.19 = (bf16[512,2560]{1,0:T(8,128)(2,1)}, bf16[512,2560]{1,0:T(8,128)(2,1)}, u32[]{:S(2)}, u32[]{:S(2)}) collective-permute-start(bf16[512,2560]{1,0:T(8,128)(2,1)} %collective-permute-done.11.refs_5_), channel_id=1, source_target_pairs={{0,1},{1,0},{2,3},{3,2},{4,5},{5,4},{6,7},{7,6},{8,9},{9,8},{10,11... | collective-permute-start | bytes 7864328 | tf_op jit(solution)/shard_map/ppermute | solution.py:272
  159.3 24.9 %collective-permute-start.20 = (bf16[512,2560]{1,0:T(8,128)(2,1)}, bf16[512,2560]{1,0:T(8,128)(2,1)}, u32[]{:S(2)}, u32[]{:S(2)}) collective-permute-start(bf16[512,2560]{1,0:T(8,128)(2,1)} %collective-permute-done.12.refs_7_), channel_id=1, source_target_pairs={{0,1},{1,0},{2,3},{3,2},{4,5},{5,4},{6,7},{7,6},{8,9},{9,8},{10,11... | collective-permute-start | bytes 7864328 | tf_op jit(solution)/shard_map/ppermute | solution.py:272
  182.4 5.3 %collective-permute-start.18 = (bf16[512,2560]{1,0:T(8,128)(2,1)}, bf16[512,2560]{1,0:T(8,128)(2,1)}, u32[]{:S(2)}, u32[]{:S(2)}) collective-permute-start(bf16[512,2560]{1,0:T(8,128)(2,1)} %constant_dynamic-update-slice_fusion.refs_3_), channel_id=1, source_target_pairs={{0,1},{1,0},{2,3},{3,2},{4,5},{5,4},{6,7},{7,6},{8,9},{9,8},{10,11... | collective-permute-start | bytes 7864328 | tf_op jit(solution)/shard_map/ppermute | solution.py:272
  225.1 55.0 %collective-permute-start.22 = (bf16[512,384]{1,0:T(8,128)(2,1)}, bf16[512,384]{1,0:T(8,128)(2,1)S(1)}, u32[]{:S(2)}, u32[]{:S(2)}) collective-permute-start(bf16[512,384]{1,0:T(8,128)(2,1)} %get-tuple-element.42), channel_id=1, source_target_pairs={{0,2},{2,0},{4,6},{6,4},{8,10},{10,8},{12,14},{14,12},{16,18},{18,... | collective-permute-start | bytes 1179656 | tf_op jit(solution)/shard_map/ppermute | solution.py:269
  226.1 67.0 %collective-permute-start.24 = (bf16[512,384]{1,0:T(8,128)(2,1)}, bf16[512,384]{1,0:T(8,128)(2,1)S(1)}, u32[]{:S(2)}, u32[]{:S(2)}) collective-permute-start(bf16[512,384]{1,0:T(8,128)(2,1)} %get-tuple-element.43), channel_id=1, source_target_pairs={{0,4},{2,6},{4,0},{6,2},{8,12},{10,14},{12,8},{14,10},{16,20},{18,... | collective-permute-start | bytes 1179656 | tf_op jit(solution)/shard_map/ppermute | solution.py:269
  226.8 66.3 %collective-permute-start.26 = (bf16[512,384]{1,0:T(8,128)(2,1)}, bf16[512,384]{1,0:T(8,128)(2,1)S(1)}, u32[]{:S(2)}, u32[]{:S(2)}) collective-permute-start(bf16[512,384]{1,0:T(8,128)(2,1)} %get-tuple-element.45), channel_id=1, source_target_pairs={{0,6},{2,4},{4,2},{6,0},{8,14},{10,12},{12,10},{14,8},{16,22},{18,... | collective-permute-start | bytes 1179656 | tf_op jit(solution)/shard_map/ppermute | solution.py:269
  280.0 13.1 %collective-permute-start.23 = (bf16[512,256]{1,0:T(8,128)(2,1)}, bf16[512,256]{1,0:T(8,128)(2,1)S(1)}, u32[]{:S(2)}, u32[]{:S(2)}) collective-permute-start(bf16[512,256]{1,0:T(8,128)(2,1)} %get-tuple-element.40), channel_id=1, source_target_pairs={{0,2},{2,0},{4,6},{6,4},{8,10},{10,8},{12,14},{14,12},{16,18},{18,... | collective-permute-start | bytes 786440 | tf_op jit(solution)/shard_map/ppermute | solution.py:269
  280.1 14.8 %collective-permute-start.25 = (bf16[512,256]{1,0:T(8,128)(2,1)}, bf16[512,256]{1,0:T(8,128)(2,1)S(1)}, u32[]{:S(2)}, u32[]{:S(2)}) collective-permute-start(bf16[512,256]{1,0:T(8,128)(2,1)} %get-tuple-element.44), channel_id=1, source_target_pairs={{0,4},{2,6},{4,0},{6,2},{8,12},{10,14},{12,8},{14,10},{16,20},{18,... | collective-permute-start | bytes 786440 | tf_op jit(solution)/shard_map/ppermute | solution.py:269
  280.2 14.7 %collective-permute-start.27 = (bf16[512,256]{1,0:T(8,128)(2,1)}, bf16[512,256]{1,0:T(8,128)(2,1)S(1)}, u32[]{:S(2)}, u32[]{:S(2)}) collective-permute-start(bf16[512,256]{1,0:T(8,128)(2,1)} %get-tuple-element.46), channel_id=1, source_target_pairs={{0,6},{2,4},{4,2},{6,0},{8,14},{10,12},{12,10},{14,8},{16,22},{18,... | collective-permute-start | bytes 786440 | tf_op jit(solution)/shard_map/ppermute | solution.py:269
  (14 other events, 98.5 us)
Sparse Core Ops, SparseCore 0:
  27.5 91.1 all-gather.2
  180.0 71.5 all-gather.4
